TPU v7x, 512 devices: a whole 4x4x16 slice. The times are simulated.
512 devices in a mesh: ctx: 64 (over z, y), head: 8 (over x, core).
Axes of the slice: x: 4, y: 4, z: 16, core: 2. Of those that a mesh axis runs over, the one named last changes fastest.
Arguments:
- tokens: bfloat16 [16384, 2048], P('ctx', 'head'), may hold values from -6 to 6
- qkv_weight: bfloat16 [2048, 3, 2048], P('ctx', None, 'head'), may hold values from -0.125 to 0.125
- out_gain: float32 [2048], P('head'), may hold values from 0.1 to 1.9
Outputs:
- attended: bfloat16 [16384, 2048], P('ctx', 'head')
All inputs are finite; a program needn't handle non-finite values.
Results may differ from a plain program's by a relative error of at most 0.001.
Values may be sent and summed in bfloat16 or wider, within the bound.
No kernel may reach another device: no remote copies, remote signals or barrier semaphores. Data moves between devices by JAX's collectives and lax.ppermute only.
A program may use at most 64 MiB of HBM per device.

v0:
```python
import math

import jax
import jax.numpy as jnp
from jax import lax
from jax.sharding import PartitionSpec as P

HD = 128


epsilon = 1e-06
highest = lax.Precision.HIGHEST


def prefix(x, axis, combine, identity):
    peers, here = (lax.axis_size(axis), lax.axis_index(axis))
    everything = jax.tree.map(lambda part: lax.all_gather(part, axis), x)
    start = jax.tree.map(
        lambda part, zero: jnp.broadcast_to(jnp.asarray(zero, part.dtype), part.shape), x, identity
    )

    def step(k, before):
        reached = k < here
        new = combine(before, jax.tree.map(lambda part: part[k], everything))
        return jax.tree.map(lambda a, b: jnp.where(reached, a, b), new, before)

    return lax.fori_loop(0, peers, step, start)


def matmul_heads(left_mat, right_mat):
    return jnp.einsum("hij,hjk->hik", left_mat, right_mat, precision=highest)


def block_terms(queries, key_rows, val_rows, prior_s, prior_m):
    rows_here = queries.shape[0]
    row_ids = lax.broadcasted_iota(jnp.int32, (rows_here, rows_here), 0)
    col_ids = lax.broadcasted_iota(jnp.int32, (rows_here, rows_here), 1)
    causal = row_ids >= col_ids
    strict = row_ids < col_ids
    scores = jnp.einsum("thd,shd->hts", queries, key_rows, precision=highest)
    lower_part = jnp.where(causal, scores, 0.0)
    pair_term = jnp.einsum("hti,hji->htj", lower_part, lower_part, precision=highest)
    query_state = jnp.einsum("thd,hde->the", queries, prior_s, precision=highest)
    cross_term = jnp.einsum("the,she->hts", query_state, queries, precision=highest)
    mixing = jnp.where(causal, pair_term + cross_term, 0.0)
    raw_out = jnp.einsum("hts,she->the", mixing, val_rows, precision=highest)
    raw_out = raw_out + jnp.einsum("thd,hde->the", queries, prior_m, precision=highest)
    local_s = jnp.einsum("thd,the->hde", key_rows, key_rows, precision=highest)
    local_c = jnp.einsum("thd,the->hde", queries, val_rows, precision=highest)
    upper_part = jnp.where(strict, scores, 0.0)
    weighted = jnp.einsum("hji,jhe->ihe", upper_part, val_rows, precision=highest)
    local_g = jnp.einsum("ihd,ihe->hde", key_rows, weighted, precision=highest)
    return (raw_out, local_s, local_c, local_g)


def combine_pairs(earlier, later_part):
    return (earlier[0] + later_part[0], earlier[1] + later_part[1])


def combine_single(earlier, later_part):
    return earlier + later_part


def body(tokens, qkv_weight, out_gain):
    gathered = lax.all_gather(tokens, "head", axis=1, tiled=True)
    rows_here = gathered.shape[0]
    col_count = qkv_weight.shape[2]
    head_count = col_count // HD
    projected = jnp.einsum(
        "tr,rch->cth",
        gathered,
        lax.all_gather(qkv_weight, "ctx", axis=0, tiled=True),
        preferred_element_type=jnp.float32,
    )
    block_len = math.gcd(rows_here, 128)
    block_count = rows_here // block_len
    projected = projected.reshape(3, block_count, block_len, head_count, HD)
    queries = projected[0]
    key_rows = projected[1]
    val_rows = projected[2]
    zeros_state = jnp.zeros((head_count, HD, HD), jnp.float32)

    def local_step(carry, pieces):
        run_s, run_c, run_g = carry
        query_blk, key_blk, val_blk = pieces
        run_m = matmul_heads(run_s, run_c) - run_g
        raw_blk, add_s, add_c, add_g = block_terms(query_blk, key_blk, val_blk, run_s, run_m)
        next_g = run_g + add_g + matmul_heads(add_s, run_c)
        return ((run_s + add_s, run_c + add_c, next_g), (raw_blk, run_c))

    totals, outputs = lax.scan(
        local_step, (zeros_state, zeros_state, zeros_state), (queries, key_rows, val_rows)
    )
    local_s, local_c, local_g = totals
    local_raw, before_c = outputs
    prior_s, prior_c = prefix((local_s, local_c), "ctx", combine_pairs, (zeros_state, zeros_state))
    own_term = local_g + matmul_heads(local_s, prior_c)
    prior_g = prefix(own_term, "ctx", combine_single, zeros_state)
    prior_m = matmul_heads(prior_s, prior_c) - prior_g
    row_ids = lax.broadcasted_iota(jnp.int32, (block_len, block_len), 0)
    col_ids = lax.broadcasted_iota(jnp.int32, (block_len, block_len), 1)
    causal = row_ids >= col_ids
    query_state = jnp.einsum("bthd,hde->bthe", queries, prior_s, precision=highest)
    cross_scores = jnp.einsum("bthe,bshe->bhts", query_state, queries, precision=highest)
    cross_scores = jnp.where(causal, cross_scores, 0.0)
    extra = jnp.einsum("bhts,bshe->bthe", cross_scores, val_rows, precision=highest)
    extra = extra + jnp.einsum("bthd,bhde->bthe", query_state, before_c, precision=highest)
    extra = extra + jnp.einsum("bthd,hde->bthe", queries, prior_m, precision=highest)
    raw_out = (local_raw + extra).reshape(rows_here, head_count, HD)
    mean_sq = jnp.mean(raw_out * raw_out, axis=-1, keepdims=True)
    normed = raw_out * lax.rsqrt(mean_sq + epsilon) * out_gain.reshape(head_count, HD)
    return normed.reshape(rows_here, col_count).astype(jnp.bfloat16)


def solution(mesh):
    in_specs = (P("ctx", "head"), P("ctx", None, "head"), P("head"))
    out_specs = P("ctx", "head")
    return jax.shard_map(body, mesh=mesh, in_specs=in_specs, out_specs=out_specs, check_vma=False)
```

profile of v0, /device:TPU:7, one launch (start us, length us, event | category | flops | bytes accessed | tf_op | source)
XLA Modules:
  0.0 796.7 jit_solution(3859147422110542077)
XLA Ops:
  8.1 36.5 %all-gather.11.cloned.1.call-done = bf16[256,2048]{1,0:T(8,128)(2,1)} async-done(((bf16[256,256]{1,0:T(8,128)(2,1)}), bf16[256,2048]{1,0:T(8,128)(2,1)}) %all-gather.11.cloned.1.call-update) | async-done | bytes 1048592 | tf_op jit(solution)/shard_map/all_gather | solution.py:65
  44.6 138.7 %all-gather.9.cloned.1.call-done = bf16[2048,3,256]{2,0,1:T(8,128)(2,1)} async-done(((bf16[32,3,256]{2,0,1:T(8,128)(2,1)}), bf16[2048,3,256]{2,0,1:T(8,128)(2,1)}) %all-gather.9.cloned.1.call-update) | async-done | bytes 3145744 | tf_op jit(solution)/shard_map/all_gather | solution.py:72
  183.3 3.2 convolution_bitcast_fusion.2
  187.0 9.6 %while.52 = (s32[]{:T(128)}, f32[2,128,128]{2,1,0:T(8,128)S(1)}, f32[2,128,128]{2,1,0:T(8,128)S(1)}, f32[2,128,128]{2,1,0:T(8,128)S(1)}, f32[2,128,2,128]{1,3,2,...) while((s32[]{:T(128)}, f32[2,128,128]{2,1,0:T(8,128)S(1)}, ...), condition=%wide.region_1.2_spmd.clone.clone, body=%wide.region_0.1_spmd.clone.sunk.clone | while | flops 604635136 | bytes 6635645 | solution.py:91
  197.9 151.8 %all-gather.13.cloned.1.call-done = f32[128,128,128]{2,1,0:T(8,128)} async-done(((f32[2,128,128]{2,1,0:T(8,128)}), f32[128,128,128]{2,1,0:T(8,128)}) %all-gather.13.cloned.1.call-update) | async-done | bytes 8388624 | tf_op jit(solution)/shard_map/all_gather | solution.py:17
  349.8 153.9 %all-gather.15.cloned.1.call-done = f32[128,128,128]{2,1,0:T(8,128)} async-done(((f32[2,128,128]{2,1,0:T(8,128)}), f32[128,128,128]{2,1,0:T(8,128)}) %all-gather.15.cloned.1.call-update) | async-done | bytes 8388624 | tf_op jit(solution)/shard_map/all_gather | solution.py:17
  503.6 69.1 %while.53 = (s32[]{:T(128)}, f32[2,128,128]{2,1,0:T(8,128)S(1)}, f32[2,128,128]{2,1,0:T(8,128)S(1)}, s32[]{:T(128)}, f32[64,2,128,128]{3,2,1,0:T(8,128)}, /*index=5*/f32[64,2,128,128]{3,2,1,0:T(8,128)}) while((s32[]{:T(128)}, f32[2,128,128]{2,1,0:T(8,128)S(1)}, f32[2,128,128]{2,1,0:T(8,128)S(1)}, s32[]{:T(128)}, ...), condition=%wide.region_3.4_spmd.clone.clone, body=%wide.region_2.3_spmd.clone.sunk.clone | while | flops 196612 | bytes 786525 | solution.py:27
  504.7 1.1 add_select_fusion.7
  505.8 1.1 add_select_fusion.7
  508.0 1.1 add_select_fusion.7
  509.0 1.1 add_select_fusion.7
  510.1 1.1 add_select_fusion.7
  511.2 1.1 add_select_fusion.7
  512.3 1.1 add_select_fusion.7
  513.4 1.1 add_select_fusion.7
  514.4 1.1 add_select_fusion.7
  515.5 1.1 add_select_fusion.7
  516.6 1.1 add_select_fusion.7
  518.8 1.1 add_select_fusion.7
  519.8 1.1 add_select_fusion.7
  522.0 1.1 add_select_fusion.7
  523.1 1.1 add_select_fusion.7
  525.2 1.1 add_select_fusion.7
  526.3 1.1 add_select_fusion.7
  528.5 1.1 add_select_fusion.7
  529.6 1.1 add_select_fusion.7
  530.6 1.1 add_select_fusion.7
  531.7 1.1 add_select_fusion.7
  532.8 1.1 add_select_fusion.7
  533.9 1.1 add_select_fusion.7
  535.0 1.1 add_select_fusion.7
  536.0 1.1 add_select_fusion.7
  537.1 1.1 add_select_fusion.7
  539.3 1.1 add_select_fusion.7
  540.4 1.1 add_select_fusion.7
  542.5 1.1 add_select_fusion.7
  543.6 1.1 add_select_fusion.7
  545.8 1.1 add_select_fusion.7
  546.8 1.1 add_select_fusion.7
  549.0 1.1 add_select_fusion.7
  550.1 1.1 add_select_fusion.7
  551.2 1.1 add_select_fusion.7
  552.3 1.1 add_select_fusion.7
  553.3 1.1 add_select_fusion.7
  554.4 1.1 add_select_fusion.7
  572.8 1.8 convolution_add_fusion.6
  577.1 148.7 %all-gather.17.cloned.1.call-done = f32[128,128,128]{2,1,0:T(8,128)} async-done(((f32[2,128,128]{2,1,0:T(8,128)}), f32[128,128,128]{2,1,0:T(8,128)}) %all-gather.17.cloned.1.call-update) | async-done | bytes 8388624 | tf_op jit(solution)/shard_map/all_gather | solution.py:17
  725.8 62.3 %while.54 = (s32[]{:T(128)}, f32[2,128,128]{2,1,0:T(8,128)S(1)}, s32[]{:T(128)}, f32[64,2,128,128]{3,2,1,0:T(8,128)}) while((s32[]{:T(128)}, f32[2,128,128]{2,1,0:T(8,128)S(1)}, s32[]{:T(128)}, f32[64,2,128,128]{3,2,1,0:T(8,128)}) %tuple.123), condition=%wide.region_5.6_spmd.clone.clone, body=%wide.region_4.5_spmd.clone.sunk.clone | while | flops 98308 | bytes 393293 | solution.py:27
  (165 shorter events, 105.3 us)
Async XLA Ops:
  6.5 38.0 %all-gather.11.cloned.1.call-start = ((), (), s32[]{:S(2)}) async-start(), calls=%async_computation.1 | async-start | bytes 1179648 | tf_op jit(solution)/shard_map/all_gather | solution.py:65
  7.3 176.0 %all-gather.9.cloned.1.call-start = ((), (), s32[]{:S(2)}) async-start(), calls=%async_computation | async-start | bytes 3194880 | tf_op jit(solution)/shard_map/all_gather | solution.py:72
  8.0 341.7 %all-gather.13.cloned.1.call-start = ((), (), s32[]{:S(2)}) async-start(), calls=%async_computation.2 | async-start | bytes 8519680 | tf_op jit(solution)/shard_map/all_gather | solution.py:17
  196.6 0.7 copy-start.1
  196.6 0.7 copy-start
  196.6 592.9 %copy-start.2 = (f32[256]{0:T(256)S(1)}, f32[256]{0:T(256)}, u32[]{:S(2)}) copy-start(f32[256]{0:T(256)} %param.11) | copy-start | bytes 3076
  197.3 306.4 %all-gather.15.cloned.1.call-start = ((), (), s32[]{:S(2)}) async-start(), calls=%async_computation.3 | async-start | bytes 8519680 | tf_op jit(solution)/shard_map/all_gather | solution.py:17
  197.8 528.0 %all-gather.17.cloned.1.call-start = ((), (), s32[]{:S(2)}) async-start(), calls=%async_computation.4 | async-start | bytes 8519680 | tf_op jit(solution)/shard_map/all_gather | solution.py:17
Sparse Core Ops, SparseCore 0:
  9.4 35.0 all-gather.10
  47.5 135.6 all-gather.8
  197.4 152.3 all-gather.12
  352.6 151.0 all-gather.14
  574.7 151.0 all-gather.16
where the time goes:
time: 807 us; the launch traced here: 797 us
  waiting for transfers between devices  632 us (78%)
  other arithmetic  129 us (16%)
  matrix products  16.5 us (2%)
  between operations  13.4 us (2%)
    all_gather x3, waiting for transfers between devices, prefix(): everything = jax.tree.map(lambda part: lax.all_gather(part, axis), x)  454 us
    all_gather x1, waiting for transfers between devices, body(): lax.all_gather(qkv_weight, 'ctx', axis=0, tiled=True)  139 us
    select_n x128, other arithmetic, step(): return jax.tree.map(lambda a, b: jnp.where(reached, a, b), new, before)  128 us
    all_gather x1, waiting for transfers between devices, body(): gathered = lax.all_gather(tokens, 'head', axis=1, tiled=True)  36.5 us
  transfers between devices with their start and end apart: 5, of which 5 were waited for; matrix products, arithmetic and copies ran while one was open for 0% of the time, Pallas kernels for 0%

commit v1 on v0

v1 whole, which is shorter than its diff:
```python
import functools

import jax
import jax.numpy as jnp
from jax import lax
from jax.experimental import pallas as pl
from jax.experimental.pallas import tpu as pltpu
from jax.sharding import Mesh, PartitionSpec as P

HD = 128
HALF = HD // 2
PACK = 96
ROWS = PACK + HD
epsilon = 1e-06
f32 = jnp.float32
bf16 = jnp.bfloat16
VM = pl.BlockSpec(memory_space=pltpu.VMEM)


def split(x):
    high = x.astype(bf16)
    return high, (x - high.astype(f32)).astype(bf16)


def mm2(a, b, ca, cb):
    dims = (((ca,), (cb,)), ((), ()))
    dot = lambda x, y: lax.dot_general(x, y, dims, preferred_element_type=f32)
    return dot(a[0], b[0]) + (dot(a[0], b[1]) + dot(a[1], b[0]))


def mm(a, b, ca=1, cb=0):
    return mm2(split(a), split(b), ca, cb)


def tril(x):
    n = x.shape[0]
    rows = lax.broadcasted_iota(jnp.int32, (n, n), 0)
    cols = lax.broadcasted_iota(jnp.int32, (n, n), 1)
    return jnp.where(rows >= cols, x, 0.0)


def pack_sym(s):
    low = jnp.concatenate([s[HALF:PACK, HALF:], s[PACK:, HALF:]], axis=1)
    return jnp.concatenate([s[:HALF], low], axis=0)


def unpack_sym(p):
    top = p[:HALF]
    corner = jnp.concatenate([p[HALF:, :HALF], p[HALF:, HALF:]], axis=0)
    low = jnp.concatenate([top[:, HALF:].T, corner], axis=1)
    return jnp.concatenate([top, low], axis=0)


def place():
    y = lax.axis_index("y")
    return lax.rem(y, 2), lax.axis_index("core")


def project_kernel(tok, own, other, q_ref, k_ref, v_ref, l_ref, blk_ref, pay_ref, wf):
    b, c = place()
    zs = own.shape[0]
    for z in range(zs):
        for f in range(2):
            near = 32 * (b if f == 0 else 1 - b)
            for part, ref in ((c, own), (1 - c, other)):
                at = pl.ds(pl.multiple_of(z * 128 + 64 * part + near, 32), 32)
                for ch in range(3):
                    wf[at, ch * HD : (ch + 1) * HD] = ref[z, f, ch]
    s_all = c_all = m_all = None
    for t in range(2):
        x = jnp.concatenate(
            [tok[(2 * (f % 2) + t) * 4 + f // 2] for f in range(8)], axis=1
        )
        proj = jnp.dot(x, wf[...], preferred_element_type=f32)
        q, k, v = proj[:, :HD], proj[:, HD : 2 * HD], proj[:, 2 * HD :]
        rows = slice(t * 256, t * 256 + 256)
        q_ref[rows], k_ref[rows], v_ref[rows] = q, k, v
        q2, k2, v2 = split(q), split(k), split(v)
        low = tril(mm2(q2, k2, 1, 1))
        l_ref[t] = low
        w = mm2(split(low), v2, 0, 0)
        s = mm2(k2, k2, 0, 0)
        cc = mm2(q2, v2, 0, 0)
        m = mm2(k2, split(w), 0, 0)
        if t == 0:
            s_all, c_all, m_all = s, cc, m
            blk_ref[0], blk_ref[1], blk_ref[2] = s, cc, m
        else:
            m_all = m_all + m + mm(s_all, cc)
            s_all, c_all = s_all + s, c_all + cc
    packed = pack_sym(s_all)
    for h in range(2):
        cols = slice(h * HALF, h * HALF + HALF)
        half = jnp.concatenate([c_all[:, cols], m_all[:, cols]], axis=1)
        for zb in range(2):
            pay_ref[2 * zb + h, :PACK] = packed
            pay_ref[2 * zb + h, PACK:] = half


def local_kernel(q_ref, v_ref, l_ref, blk_ref, raw_ref):
    for t in range(2):
        rows = slice(t * 256, t * 256 + 256)
        low = split(l_ref[t])
        pair = mm2(low, low, 1, 1)
        if t == 1:
            q2 = split(q_ref[rows])
            qs = mm2(q2, split(blk_ref[0]), 1, 0)
            pair = pair + mm2(split(qs), q2, 1, 1)
        raw = mm(tril(pair), v_ref[rows])
        if t == 1:
            raw = raw + mm2(q2, split(blk_ref[2]), 1, 0)
        raw_ref[rows] = raw


def pair_kernel(got, pay_ref, in_ref, s_in_ref):
    _, c = place()
    zb = lax.rem(lax.axis_index("z"), 2)
    pos = 2 * zb + c
    s = jnp.zeros((PACK, HD), f32)
    cm = jnp.zeros((HD, HD), f32)
    s_in = s
    before = [cm, cm]
    left = lax.broadcasted_iota(jnp.int32, (HD, HD), 1) < HALF
    for i in range(4):
        s_in = jnp.where(pos == i, s, s_in)
        before[i % 2] = jnp.where(zb == i // 2, cm, before[i % 2])
        new = got[i, PACK:]
        if i:
            cross = mm(unpack_sym(s), new[:, :HALF])
            cross = jnp.concatenate([jnp.zeros_like(cross), cross], axis=1)
            cm = cm + new + cross
        else:
            cm = new
        s = s + got[i, :PACK]
    pay_ref[:PACK] = s
    pay_ref[PACK:] = cm
    in_ref[0], in_ref[1] = before
    s_in_ref[...] = s_in


def prior_kernel(got, in_ref, s_in_ref, s_ref, keep_ref, send_ref):
    _, c = place()
    pair = lax.div(lax.axis_index("z"), 2)
    n = got.shape[0]
    s = jnp.zeros((PACK, HD), f32)
    m = jnp.zeros((HD, HALF), f32)
    lefts, rights = [], []
    for p in range(n - 1):
        live = p < pair
        if p:
            lefts.append(unpack_sym(s))
            rights.append(jnp.where(live, got[p, PACK:, :HALF], 0.0))
        m = m + jnp.where(live, got[p, PACK:, HALF:], 0.0)
        s = s + jnp.where(live, got[p, :PACK], 0.0)
    m = m + mm(jnp.concatenate(lefts, axis=1), jnp.concatenate(rights, axis=0))
    full = unpack_sym(s)
    both = jnp.concatenate([in_ref[0][:, :HALF], in_ref[1][:, :HALF]], axis=1)
    cross = mm(full, both)
    m0 = m + in_ref[0][:, HALF:] + cross[:, :HALF]
    m1 = m + in_ref[1][:, HALF:] + cross[:, HALF:]
    s_ref[...] = full + unpack_sym(s_in_ref[...])
    keep_ref[...] = jnp.where(c == 0, m0, m1)
    send_ref[...] = jnp.where(c == 0, m1, m0)


def cross_kernel(q_ref, v_ref, raw_ref, blk_ref, s_ref, out_ref):
    s2 = split(s_ref[...])
    for t in range(2):
        rows = slice(t * 256, t * 256 + 256)
        q2 = split(q_ref[rows])
        qs = split(mm2(q2, s2, 1, 0))
        scores = tril(mm2(qs, q2, 1, 1))
        raw = raw_ref[rows] + mm(scores, v_ref[rows])
        if t == 1:
            raw = raw + mm2(qs, split(blk_ref[1]), 1, 0)
        out_ref[rows] = raw


def final_kernel(q_ref, raw_ref, keep_ref, other_ref, gain_ref, gain_far_ref, out_ref):
    b, c = place()
    keep, other = keep_ref[...], other_ref[...]
    m2 = split(
        jnp.concatenate(
            [jnp.where(c == 0, keep, other), jnp.where(c == 0, other, keep)], axis=1
        )
    )
    y = lax.axis_index("y")
    gain = jnp.where(lax.div(y, 2) == c, gain_ref[...], gain_far_ref[...])
    gain = jnp.where(b == 0, gain[0:1], gain[1:2])
    for t in range(2):
        rows = slice(t * 256, t * 256 + 256)
        raw = raw_ref[rows] + mm2(split(q_ref[rows]), m2, 1, 0)
        mean_sq = jnp.mean(raw * raw, axis=-1, keepdims=True)
        out = raw * lax.rsqrt(mean_sq + epsilon) * gain
        out_ref[b if t == 0 else 1 - b] = out.astype(bf16)


def call(kernel, outs, flops, moved, scratch=()):
    return pl.pallas_call(
        kernel,
        out_shape=outs,
        scratch_shapes=list(scratch),
        compiler_params=pltpu.CompilerParams(vmem_limit_bytes=32 * 2**20),
        cost_estimate=pl.CostEstimate(flops=flops, bytes_accessed=moved, transcendentals=0),
    )


def swap_perm(flip):
    return [
        ((2 * a + b) * 2 + c, (2 * c + (b ^ flip)) * 2 + a)
        for a in range(2)
        for b in range(2)
        for c in range(2)
    ]


def body(zs, tokens, weight, gain):
    shape = jax.ShapeDtypeStruct
    b = lax.rem(lax.axis_index("y"), 2)
    yc = ("y", "core")
    first, second = weight[:, :, :HD], weight[:, :, HD:]
    same = jnp.where(b == 0, first, second).transpose(1, 0, 2)
    flip = jnp.where(b == 0, second, first).transpose(1, 0, 2)
    same = lax.ppermute(same, yc, swap_perm(0))
    flip = lax.ppermute(flip, yc, swap_perm(1))
    moved = lax.ppermute(tokens, yc, swap_perm(0))
    moved, same, flip = lax.optimization_barrier((moved, same, flip))
    everything = jnp.broadcast_to(moved[None], (16,) + moved.shape)
    tok = lax.all_to_all(everything, ("y", "x"), 0, 0)
    own = lax.all_gather(jnp.stack([same, flip]), "z")
    core_swap = [(0, 1), (1, 0)]
    other = lax.ppermute(own, "core", core_swap)
    rows = shape((512, HD), f32)
    mats = lambda n: shape((n, HD, HD), f32)
    q, k, v, low, blk, pay = call(
        project_kernel,
        (rows, rows, rows, shape((2, 256, 256), f32), mats(3), shape((4, ROWS, HD), f32)),
        1200 * 10**6,
        8 * 10**6,
        [pltpu.VMEM((zs * 128, 3 * HD), bf16)],
    )(tok, own, other)
    groups = [[(2 * p + i) * 2 + j for i in range(2) for j in range(2)] for p in range(zs // 2)]
    got = lax.all_to_all(pay, ("z", "core"), 0, 0, axis_index_groups=groups)
    gain, pay = lax.optimization_barrier((gain, pay))
    gain = gain.reshape(2, HD)
    gain_far = lax.ppermute(gain, "core", core_swap)
    raw = call(local_kernel, rows, 600 * 10**6, 4 * 10**6)(q, v, low, blk)
    total, inner, s_in = call(
        pair_kernel, (shape((ROWS, HD), f32), mats(2), shape((PACK, HD), f32)), 10**8, 10**6
    )(got)
    groups = [[2 * p + i for p in range(zs // 2)] for i in range(2)]
    totals = lax.all_gather(total, "z", axis_index_groups=groups)
    s, keep, send = call(
        prior_kernel, (shape((HD, HD), f32), shape((HD, HALF), f32), shape((HD, HALF), f32)), 10**8, 10**6
    )(totals, inner, s_in)
    other_m = lax.ppermute(send, "core", core_swap)
    raw = call(cross_kernel, rows, 500 * 10**6, 2 * 10**6)(q, v, raw, blk, s)
    out = call(final_kernel, shape((2, 256, HD), bf16), 10**8, 10**6)(
        q, raw, keep, other_m, gain, gain_far
    )
    near = lax.ppermute(out[0], yc, swap_perm(0))
    far = lax.ppermute(out[1], yc, swap_perm(1))
    left = jnp.where(b == 0, near, far)
    right = jnp.where(b == 0, far, near)
    return jnp.concatenate([left, right], axis=1)


def solution(mesh):
    zs = mesh.shape["ctx"] // 4
    fine = Mesh(mesh.devices.reshape(zs, 4, 4, 2), ("z", "y", "x", "core"))
    ctx, head = ("z", "y"), ("x", "core")
    return jax.shard_map(
        functools.partial(body, zs),
        mesh=fine,
        in_specs=(P(ctx, head), P(ctx, None, head), P(head)),
        out_specs=P(ctx, head),
        check_vma=False,
    )
```

time: 807 us -> 139 us (0.17); the launches traced: 797 us -> 139 us
  waiting for transfers between devices: 632 us -> 8.43 us
  other arithmetic: 129 us -> 1.46 us
  blocking collectives: 0 us -> 62.8 us
  starting transfers between devices: 0.16 us -> 50.1 us
  matrix products: 16.5 us -> 0 us
  between operations: 13.4 us -> 0.17 us
  Pallas kernels: 0 us -> 8.78 us
    all_gather x5 -> x0, waiting for transfers between devices: 630 us -> none  [the longest x3 454 us: prefix(): everything = jax.tree.map(lambda part: lax.all_gather(part, axis), x)]
    select_n x128 -> x1, other arithmetic: 128 us -> 0.01 us  [body(): left = jnp.where(b == 0, near, far)]
    all_gather x0 -> x2, blocking collectives: none -> 62.8 us  [the longest x1 34.2 us: body(): own = lax.all_gather(jnp.stack([same, flip]), 'z')]
    ppermute x0 -> x8, starting transfers between devices: none -> 42 us  [the longest x1 11 us: body(): other = lax.ppermute(own, 'core', core_swap)]
    dot_general x32 -> x0, matrix products: 16.5 us -> none  [the longest x1 3.19 us: body(): jnp.einsum('tr,rch->cth', gathered, lax.all_gather(qkv_weight, 'ctx', axi...]
    pallas_call x0 -> x6, Pallas kernels: none -> 8.78 us  [the longest x1 4.27 us: body(): call(project_kernel, (rows, rows, rows, shape((2, 256, 256), f32), mats(3...]
  transfers between devices with their start and end apart: 5 -> 10, of which waited for: 5 -> 4; matrix products, arithmetic and copies ran while one was open for 0% -> 1% of each run, Pallas kernels for 0% -> 3%
where the time goes in v1:
time: 139 us
  blocking collectives  62.8 us (45%)
  starting transfers between devices  50.1 us (36%)
  Pallas kernels  8.78 us (6%)
  waiting for transfers between devices  8.43 us (6%)
  local copies, waits for them, and re-layouts  7.01 us (5%)
  other arithmetic  1.46 us (1%)
    all_gather x1, blocking collectives, body(): own = lax.all_gather(jnp.stack([same, flip]), 'z')  34.2 us
    all_gather x1, blocking collectives, body(): totals = lax.all_gather(total, 'z', axis_index_groups=groups)  28.6 us
    ppermute x1, starting transfers between devices, body(): other = lax.ppermute(own, 'core', core_swap)  11 us
    ppermute x1, starting transfers between devices, body(): near = lax.ppermute(out[0], yc, swap_perm(0))  7.07 us
    ppermute x1, starting transfers between devices, body(): other_m = lax.ppermute(send, 'core', core_swap)  6.24 us
    unnamed x16, local copies, waits for them, and re-layouts  5.47 us
    ppermute x1, starting transfers between devices, body(): moved = lax.ppermute(tokens, yc, swap_perm(0))  5.37 us
    ppermute x1, starting transfers between devices, body(): flip = lax.ppermute(flip, yc, swap_perm(1))  4.97 us
  transfers between devices with their start and end apart: 10, of which 4 were waited for; matrix products, arithmetic and copies ran while one was open for 1% of the time, Pallas kernels for 3%

profile of v1, /device:TPU:7, one launch (start us, length us, event | category | flops | bytes accessed | tf_op | source)
XLA Modules:
  0.0 138.8 jit_solution(18070092420972720918)
XLA Ops:
  0.0 5.4 %collective-permute-start = (bf16[256,256]{1,0:T(8,128)(2,1)}, bf16[256,256]{1,0:T(8,128)(2,1)S(1)}, u32[]{:S(2)}, u32[]{:S(2)}) collective-permute-start(bf16[256,256]{1,0:T(8,128)(2,1)} %param.3), channel_id=1, source_target_pairs={{0,0},{1,16},{8,8},{9,24},{16,1},{17,17},{24,9},{25,25},{2,2},{3,1... | collective-permute-start | bytes 393224 | tf_op jit(solution)/shard_map/ppermute | solution.py:226
  5.4 0.8 select_bitcast_fusion
  6.2 1.9 %collective-permute-start.1 = (bf16[3,32,128]{2,1,0:T(8,128)(2,1)S(1)}, bf16[3,32,128]{2,1,0:T(8,128)(2,1)S(1)}, u32[]{:S(2)}, u32[]{:S(2)}) collective-permute-start(bf16[3,32,128]{2,1,0:T(8,128)(2,1)S(1)} %get-tuple-element.40), channel_id=1, source_target_pairs={{0,0},{1,16},{8,8},{9,24},{16,1},{17,17},{24,9},{25,25},{2,2},{3,1... | collective-permute-start | bytes 73736 | tf_op jit(solution)/shard_map/ppermute | solution.py:224
  8.1 5.0 %collective-permute-start.2 = (bf16[3,32,128]{2,1,0:T(8,128)(2,1)S(1)}, bf16[3,32,128]{2,1,0:T(8,128)(2,1)S(1)}, u32[]{:S(2)}, u32[]{:S(2)}) collective-permute-start(bf16[3,32,128]{2,1,0:T(8,128)(2,1)S(1)} %get-tuple-element.39), channel_id=1, source_target_pairs={{0,8},{1,24},{8,0},{9,16},{16,9},{17,25},{24,1},{25,17},{2,10},{3,... | collective-permute-start | bytes 73736 | tf_op jit(solution)/shard_map/ppermute | solution.py:225
  13.0 0.0 collective-permute-done.1
  13.1 1.5 %collective-permute-done.2 = bf16[3,32,128]{2,1,0:T(8,128)(2,1)S(1)} collective-permute-done((bf16[3,32,128]{2,1,0:T(8,128)(2,1)S(1)}, bf16[3,32,128]{2,1,0:T(8,128)(2,1)S(1)}, u32[]{:S(2)}, u32[]{:S(2)}) %collective-permute-start.2) | collective-permute-done | bytes 24608 | tf_op jit(solution)/shard_map/ppermute | solution.py:225
  14.5 0.0 collective-permute-done
  14.5 1.5 %broadcast_in_dim.2 = bf16[16,256,256]{2,1,0:T(8,128)(2,1)} broadcast(bf16[256,256]{1,0:T(8,128)(2,1)S(1)} %collective-permute-done), dimensions={1,2} | broadcast | bytes 2228224 | tf_op jit(solution)/shard_map/broadcast_in_dim | solution.py:228
  16.1 4.2 %all-to-all-start = ((bf16[16,256,256]{2,1,0:T(8,128)(2,1)}), bf16[16,256,256]{2,1,0:T(8,128)(2,1)S(1)}, u32[]{:S(2)}, u32[]{:S(2)}) async-start(bf16[16,256,256]{2,1,0:T(8,128)(2,1)} %broadcast_in_dim.2), calls=%async_computation | async-start | bytes 4194304 | tf_op jit(solution)/shard_map/all_to_all | solution.py:229
  20.3 34.2 %all-gather = bf16[32,3,32,128]{3,2,1,0:T(8,128)(2,1)S(1)} all-gather(bf16[2,3,32,128]{3,2,1,0:T(8,128)(2,1)S(1)} %pad_maximum_fusion.1), channel_id=2, replica_groups=mesh['z'=16,'y'=4,'x'=4,'core'=2] {'z'}, dimensions={0}, use_global_device_ids=true | all-gather | bytes 835584 | tf_op jit(solution)/shard_map/all_gather | solution.py:230
  54.5 0.0 copy-start
  54.5 11.0 %collective-permute-start.3 = (bf16[16,2,3,32,128]{4,3,2,1,0:T(8,128)(2,1)S(1)}, bf16[16,2,3,32,128]{4,3,2,1,0:T(8,128)(2,1)S(1)}, u32[]{:S(2)}, u32[]{:S(2)}) collective-permute-start(bf16[16,2,3,32,128]{4,3,2,1,0:T(8,128)(2,1)S(1)} %bitcast.14), channel_id=1, source_target_pairs={{0,1},{1,0},{2,3},{3,2},{4,5},{5,4},{6,7},{7,6},{8,9},{9,8},{10,11... | collective-permute-start | bytes 2359304 | tf_op jit(solution)/shard_map/ppermute | solution.py:232
  65.5 1.9 %collective-permute-done.3.other = bf16[16,2,3,32,128]{4,3,2,1,0:T(8,128)(2,1)S(1)} collective-permute-done((bf16[16,2,3,32,128]{4,3,2,1,0:T(8,128)(2,1)S(1)}, bf16[16,2,3,32,128]{4,3,2,1,0:T(8,128)(2,1)S(1)}, u32[]{:S(2)}, u32[]{:S(2)}) %collective-permute-start.3) | collective-permute-done | bytes 786464 | tf_op jit(solution)/shard_map/ppermute | solution.py:232
  67.4 0.0 copy-start.1
  67.4 0.9 copy-done.1
  68.3 0.0 all-to-all-done.tok
  68.3 0.0 copy-start.2
  68.3 1.1 copy-done.2
  69.4 4.3 %shard_map.37 = (f32[512,128]{1,0:T(8,128)S(1)}, f32[512,128]{1,0:T(8,128)}, f32[512,128]{1,0:T(8,128)S(1)}, f32[2,256,256]{2,1,0:T(8,128)S(1)}, f32[3,128,128]{2,1,0:T(8,128)S(1)}, /*index=5*/f32[4,224,128]{2,1,0:T(8,128)}) custom-call(bf16[16,256,256]{2,1,0:T(8,128)(2,1)S(1)} %all-to-all-done.tok, bf16[16,2,3,32,128]{4,3,2,1,0:T(8,128)(2,1)S(1)} %bitcast.15, ...), custom_call_target="tpu_custom_call" | custom-call | flops 1200000000 | bytes 8000000 | tf_op jit(solution)/shard_map/pallas_call | solution.py:235
  73.7 0.0 copy-start.3
  73.7 0.8 copy-done.3
  74.5 0.0 copy-start.5
  74.5 0.7 copy-done.5
  75.2 3.8 %all-to-all-start.1 = ((f32[4,224,128]{2,1,0:T(8,128)}), f32[4,224,128]{2,1,0:T(8,128)S(1)}, u32[]{:S(2)}, u32[]{:S(2)}) async-start(f32[4,224,128]{2,1,0:T(8,128)} %get-tuple-element.27), calls=%async_computation.1 | async-start | bytes 917504 | tf_op jit(solution)/shard_map/all_to_all | solution.py:243
  79.0 0.0 copy-done
  79.0 2.0 %collective-permute-start.5 = (f32[2,128]{1,0:T(2,128)S(1)}, f32[2,128]{1,0:T(2,128)S(1)}, u32[]{:S(2)}, u32[]{:S(2)}) collective-permute-start(f32[2,128]{1,0:T(2,128)S(1)} %bitcast.16), channel_id=1, source_target_pairs={{0,1},{1,0},{2,3},{3,2},{4,5},{5,4},{6,7},{7,6},{8,9},{9,8},{10,11... | collective-permute-start | bytes 3080 | tf_op jit(solution)/shard_map/ppermute | solution.py:246
  80.9 0.0 copy-start.4
  81.0 1.0 copy-done.4
  82.0 0.0 copy-start.6
  82.0 0.9 copy-done.6
  82.9 0.0 copy-start.7
  82.9 1.4 %shard_map.38.raw_ref = f32[512,128]{1,0:T(8,128)S(1)} custom-call(f32[512,128]{1,0:T(8,128)S(1)} %get-tuple-element.23.q_ref, f32[512,128]{1,0:T(8,128)S(1)} %get-tuple-element.24.v_ref, f32[2,256,256]{2,1,0:T(8,128)S(1)} %copy-done.4, f32[3,128,128]{2,1,0:T(8,128)S(1)} %copy-done.6), custom_call_target="tpu_custom_call" | custom-call | flops 600000000 | bytes 4000000 | tf_op jit(solution)/shard_map/pallas_call | solution.py:247
  84.3 1.8 %all-to-all-done.1.got = f32[4,224,128]{2,1,0:T(8,128)S(1)} async-done(((f32[4,224,128]{2,1,0:T(8,128)}), f32[4,224,128]{2,1,0:T(8,128)S(1)}, u32[]{:S(2)}, u32[]{:S(2)}) %all-to-all-start.1) | async-done | bytes 458784 | tf_op jit(solution)/shard_map/all_to_all | solution.py:243
  86.1 0.5 shard_map.39
  86.6 28.6 %all-gather.1 = f32[1792,128]{1,0:T(8,128)S(1)} all-gather(f32[224,128]{1,0:T(8,128)S(1)} %get-tuple-element.28), channel_id=3, replica_groups={{0,64,128,192,256,320,384,448},{32,96,160,224,288,352,416,480},{1,65,12..., dimensions={0}, use_global_device_ids=true | all-gather | bytes 1032192 | tf_op jit(solution)/shard_map/all_gather | solution.py:252
  115.2 0.8 shard_map.40
  116.0 6.2 %collective-permute-start.4 = (f32[128,64]{1,0:T(8,128)S(1)}, f32[128,64]{1,0:T(8,128)S(1)}, u32[]{:S(2)}, u32[]{:S(2)}) collective-permute-start(f32[128,64]{1,0:T(8,128)S(1)} %get-tuple-element.33), channel_id=1, source_target_pairs={{0,1},{1,0},{2,3},{3,2},{4,5},{5,4},{6,7},{7,6},{8,9},{9,8},{10,11... | collective-permute-start | bytes 98312 | tf_op jit(solution)/shard_map/ppermute | solution.py:256
  122.3 0.0 copy-done.7
  122.3 1.4 %shard_map.41.raw_ref = f32[512,128]{1,0:T(8,128)S(1)} custom-call(f32[512,128]{1,0:T(8,128)S(1)} %get-tuple-element.23.q_ref, f32[512,128]{1,0:T(8,128)S(1)} %get-tuple-element.24.v_ref, f32[512,128]{1,0:T(8,128)S(1)} %shard_map.38.raw_ref, f32[3,128,128]{2,1,0:T(8,128)S(1)} %copy-done.7, f32[128,128]{1,0:T(8,128)S(1)} %get-tuple-element.31.s_ref), custom_call_target="tpu_custom_call" | custom-call | flops 500000000 | bytes 2000000 | tf_op jit(solution)/shard_map/pallas_call | solution.py:257
  123.7 0.0 collective-permute-done.5.gain_far_ref
  123.7 0.0 collective-permute-done.4.other_ref
  123.7 0.5 shard_map.42
  124.2 7.1 %collective-permute-start.6 = (bf16[256,128]{1,0:T(8,128)(2,1)S(1)}, bf16[256,128]{1,0:T(8,128)(2,1)S(1)}, u32[]{:S(2)}, u32[]{:S(2)}) collective-permute-start(bf16[256,128]{1,0:T(8,128)(2,1)S(1)} %get-tuple-element.37), channel_id=1, source_target_pairs={{0,0},{1,16},{8,8},{9,24},{16,1},{17,17},{24,9},{25,25},{2,2},{3,1... | collective-permute-start | bytes 196616 | tf_op jit(solution)/shard_map/ppermute | solution.py:261
  131.3 3.5 %collective-permute-start.7 = (bf16[256,128]{1,0:T(8,128)(2,1)S(1)}, bf16[256,128]{1,0:T(8,128)(2,1)S(1)}, u32[]{:S(2)}, u32[]{:S(2)}) collective-permute-start(bf16[256,128]{1,0:T(8,128)(2,1)S(1)} %get-tuple-element.38), channel_id=1, source_target_pairs={{0,8},{1,24},{8,0},{9,16},{16,9},{17,25},{24,1},{25,17},{2,10},{3,... | collective-permute-start | bytes 196616 | tf_op jit(solution)/shard_map/ppermute | solution.py:262
  134.8 0.0 collective-permute-done.6
  134.8 3.2 %collective-permute-done.7 = bf16[256,128]{1,0:T(8,128)(2,1)S(1)} collective-permute-done((bf16[256,128]{1,0:T(8,128)(2,1)S(1)}, bf16[256,128]{1,0:T(8,128)(2,1)S(1)}, u32[]{:S(2)}, u32[]{:S(2)}) %collective-permute-start.7) | collective-permute-done | bytes 65568 | tf_op jit(solution)/shard_map/ppermute | solution.py:262
  138.1 0.7 pad_maximum_fusion
  (3 shorter events, 0.0 us)
Async XLA Ops:
  0.0 14.5 %collective-permute-start = (bf16[256,256]{1,0:T(8,128)(2,1)}, bf16[256,256]{1,0:T(8,128)(2,1)S(1)}, u32[]{:S(2)}, u32[]{:S(2)}) collective-permute-start(bf16[256,256]{1,0:T(8,128)(2,1)} %param.3), channel_id=1, source_target_pairs={{0,0},{1,16},{8,8},{9,24},{16,1},{17,17},{24,9},{25,25},{2,2},{3,1... | collective-permute-start | bytes 393224 | tf_op jit(solution)/shard_map/ppermute | solution.py:226
  6.2 6.9 %collective-permute-start.1 = (bf16[3,32,128]{2,1,0:T(8,128)(2,1)S(1)}, bf16[3,32,128]{2,1,0:T(8,128)(2,1)S(1)}, u32[]{:S(2)}, u32[]{:S(2)}) collective-permute-start(bf16[3,32,128]{2,1,0:T(8,128)(2,1)S(1)} %get-tuple-element.40), channel_id=1, source_target_pairs={{0,0},{1,16},{8,8},{9,24},{16,1},{17,17},{24,9},{25,25},{2,2},{3,1... | collective-permute-start | bytes 73736 | tf_op jit(solution)/shard_map/ppermute | solution.py:224
  8.1 6.5 %collective-permute-start.2 = (bf16[3,32,128]{2,1,0:T(8,128)(2,1)S(1)}, bf16[3,32,128]{2,1,0:T(8,128)(2,1)S(1)}, u32[]{:S(2)}, u32[]{:S(2)}) collective-permute-start(bf16[3,32,128]{2,1,0:T(8,128)(2,1)S(1)} %get-tuple-element.39), channel_id=1, source_target_pairs={{0,8},{1,24},{8,0},{9,16},{16,9},{17,25},{24,1},{25,17},{2,10},{3,... | collective-permute-start | bytes 73736 | tf_op jit(solution)/shard_map/ppermute | solution.py:225
  16.1 52.2 %all-to-all-start = ((bf16[16,256,256]{2,1,0:T(8,128)(2,1)}), bf16[16,256,256]{2,1,0:T(8,128)(2,1)S(1)}, u32[]{:S(2)}, u32[]{:S(2)}) async-start(bf16[16,256,256]{2,1,0:T(8,128)(2,1)} %broadcast_in_dim.2), calls=%async_computation | async-start | bytes 4194304 | tf_op jit(solution)/shard_map/all_to_all | solution.py:229
  54.5 24.5 %copy-start = (f32[256]{0:T(256)S(1)}, f32[256]{0:T(256)}, u32[]{:S(2)}) copy-start(f32[256]{0:T(256)} %param.5) | copy-start | bytes 3076
  54.5 12.9 %collective-permute-start.3 = (bf16[16,2,3,32,128]{4,3,2,1,0:T(8,128)(2,1)S(1)}, bf16[16,2,3,32,128]{4,3,2,1,0:T(8,128)(2,1)S(1)}, u32[]{:S(2)}, u32[]{:S(2)}) collective-permute-start(bf16[16,2,3,32,128]{4,3,2,1,0:T(8,128)(2,1)S(1)} %bitcast.14), channel_id=1, source_target_pairs={{0,1},{1,0},{2,3},{3,2},{4,5},{5,4},{6,7},{7,6},{8,9},{9,8},{10,11... | collective-permute-start | bytes 2359304 | tf_op jit(solution)/shard_map/ppermute | solution.py:232
  67.4 0.9 copy-start.1
  68.3 1.1 copy-start.2
  73.7 0.8 copy-start.3
  74.5 0.7 copy-start.5
  75.2 11.0 %all-to-all-start.1 = ((f32[4,224,128]{2,1,0:T(8,128)}), f32[4,224,128]{2,1,0:T(8,128)S(1)}, u32[]{:S(2)}, u32[]{:S(2)}) async-start(f32[4,224,128]{2,1,0:T(8,128)} %get-tuple-element.27), calls=%async_computation.1 | async-start | bytes 917504 | tf_op jit(solution)/shard_map/all_to_all | solution.py:243
  79.0 44.7 %collective-permute-start.5 = (f32[2,128]{1,0:T(2,128)S(1)}, f32[2,128]{1,0:T(2,128)S(1)}, u32[]{:S(2)}, u32[]{:S(2)}) collective-permute-start(f32[2,128]{1,0:T(2,128)S(1)} %bitcast.16), channel_id=1, source_target_pairs={{0,1},{1,0},{2,3},{3,2},{4,5},{5,4},{6,7},{7,6},{8,9},{9,8},{10,11... | collective-permute-start | bytes 3080 | tf_op jit(solution)/shard_map/ppermute | solution.py:246
  80.9 1.0 copy-start.4
  82.0 0.9 copy-start.6
  82.9 39.4 %copy-start.7 = (f32[3,128,128]{2,1,0:T(8,128)S(1)}, f32[3,128,128]{2,1,0:T(8,128)}, u32[]{:S(2)}) copy-start(f32[3,128,128]{2,1,0:T(8,128)} %copy-done.5) | copy-start | bytes 589828
  116.0 7.7 %collective-permute-start.4 = (f32[128,64]{1,0:T(8,128)S(1)}, f32[128,64]{1,0:T(8,128)S(1)}, u32[]{:S(2)}, u32[]{:S(2)}) collective-permute-start(f32[128,64]{1,0:T(8,128)S(1)} %get-tuple-element.33), channel_id=1, source_target_pairs={{0,1},{1,0},{2,3},{3,2},{4,5},{5,4},{6,7},{7,6},{8,9},{9,8},{10,11... | collective-permute-start | bytes 98312 | tf_op jit(solution)/shard_map/ppermute | solution.py:256
  124.2 10.6 %collective-permute-start.6 = (bf16[256,128]{1,0:T(8,128)(2,1)S(1)}, bf16[256,128]{1,0:T(8,128)(2,1)S(1)}, u32[]{:S(2)}, u32[]{:S(2)}) collective-permute-start(bf16[256,128]{1,0:T(8,128)(2,1)S(1)} %get-tuple-element.37), channel_id=1, source_target_pairs={{0,0},{1,16},{8,8},{9,24},{16,1},{17,17},{24,9},{25,25},{2,2},{3,1... | collective-permute-start | bytes 196616 | tf_op jit(solution)/shard_map/ppermute | solution.py:261
  131.3 6.8 %collective-permute-start.7 = (bf16[256,128]{1,0:T(8,128)(2,1)S(1)}, bf16[256,128]{1,0:T(8,128)(2,1)S(1)}, u32[]{:S(2)}, u32[]{:S(2)}) collective-permute-start(bf16[256,128]{1,0:T(8,128)(2,1)S(1)} %get-tuple-element.38), channel_id=1, source_target_pairs={{0,8},{1,24},{8,0},{9,16},{16,9},{17,25},{24,1},{25,17},{2,10},{3,... | collective-permute-start | bytes 196616 | tf_op jit(solution)/shard_map/ppermute | solution.py:262

commit v2 on v1

--- a/solution.py
+++ b/solution.py
@@ -56,28 +56,37 @@
     return lax.rem(y, 2), lax.axis_index("core")
 
 
-def project_kernel(tok, own, other, q_ref, k_ref, v_ref, l_ref, blk_ref, pay_ref, wf):
+def ring():
+    return lax.rem(lax.axis_index("z") + lax.axis_index("core"), 2)
+
+
+def ring_groups(zs):
+    return [[z * 2 + (z + g) % 2 for z in range(zs)] for g in range(2)]
+
+
+def project_kernel(mine, tok, own, out_ref, wf):
     b, c = place()
-    zs = own.shape[0]
-    for z in range(zs):
+    half = c if mine else 1 - c
+    for z in range(own.shape[0]):
+        zh, z1, z0 = z // 4, z // 2 % 2, z % 2
         for f in range(2):
             near = 32 * (b if f == 0 else 1 - b)
-            for part, ref in ((c, own), (1 - c, other)):
-                at = pl.ds(pl.multiple_of(z * 128 + 64 * part + near, 32), 32)
-                for ch in range(3):
-                    wf[at, ch * HD : (ch + 1) * HD] = ref[z, f, ch]
-    s_all = c_all = m_all = None
-    for t in range(2):
-        x = jnp.concatenate(
-            [tok[(2 * (f % 2) + t) * 4 + f // 2] for f in range(8)], axis=1
-        )
-        proj = jnp.dot(x, wf[...], preferred_element_type=f32)
+            at = pl.ds(pl.multiple_of(zh * 256 + z0 * 128 + 64 * z1 + near, 32), 32)
+            for ch in range(3):
+                wf[at, ch * HD : (ch + 1) * HD] = own[z, f, ch]
+    for t in range(2):
+        x = jnp.concatenate([tok[8 * half + 4 * t + f] for f in range(4)], axis=1)
+        out_ref[256 * t : 256 * t + 256] = jnp.dot(x, wf[...], preferred_element_type=f32)
+
+
+def moment_kernel(keep, got, q_ref, k_ref, v_ref, blk_ref, pay_ref):
+    for t in range(2):
+        rows = slice(t * 256, t * 256 + 256)
+        proj = keep[rows] + got[rows]
         q, k, v = proj[:, :HD], proj[:, HD : 2 * HD], proj[:, 2 * HD :]
-        rows = slice(t * 256, t * 256 + 256)
         q_ref[rows], k_ref[rows], v_ref[rows] = q, k, v
         q2, k2, v2 = split(q), split(k), split(v)
         low = tril(mm2(q2, k2, 1, 1))
-        l_ref[t] = low
         w = mm2(split(low), v2, 0, 0)
         s = mm2(k2, k2, 0, 0)
         cc = mm2(q2, v2, 0, 0)
@@ -93,17 +102,18 @@
         cols = slice(h * HALF, h * HALF + HALF)
         half = jnp.concatenate([c_all[:, cols], m_all[:, cols]], axis=1)
         for zb in range(2):
-            pay_ref[2 * zb + h, :PACK] = packed
-            pay_ref[2 * zb + h, PACK:] = half
-
-
-def local_kernel(q_ref, v_ref, l_ref, blk_ref, raw_ref):
+            slot = 2 * zb + (zb + h) % 2
+            pay_ref[slot, :PACK] = packed
+            pay_ref[slot, PACK:] = half
+
+
+def local_kernel(q_ref, k_ref, v_ref, blk_ref, raw_ref):
     for t in range(2):
         rows = slice(t * 256, t * 256 + 256)
-        low = split(l_ref[t])
+        q2 = split(q_ref[rows])
+        low = split(tril(mm2(q2, split(k_ref[rows]), 1, 1)))
         pair = mm2(low, low, 1, 1)
         if t == 1:
-            q2 = split(q_ref[rows])
             qs = mm2(q2, split(blk_ref[0]), 1, 0)
             pair = pair + mm2(split(qs), q2, 1, 1)
         raw = mm(tril(pair), v_ref[rows])
@@ -112,7 +122,7 @@
         raw_ref[rows] = raw
 
 
-def pair_kernel(got, pay_ref, in_ref, s_in_ref):
+def pair_kernel(got, pay_ref, in_ref, s_in_ref, all_ref):
     _, c = place()
     zb = lax.rem(lax.axis_index("z"), 2)
     pos = 2 * zb + c
@@ -132,8 +142,9 @@
         else:
             cm = new
         s = s + got[i, :PACK]
-    pay_ref[:PACK] = s
-    pay_ref[PACK:] = cm
+    all_ref[:PACK] = s
+    all_ref[PACK:] = cm
+    pay_ref[...] = all_ref[pl.ds(pl.multiple_of(zb * (ROWS // 2), 8), ROWS // 2)]
     in_ref[0], in_ref[1] = before
     s_in_ref[...] = s_in
 
@@ -176,12 +187,13 @@
         out_ref[rows] = raw
 
 
-def final_kernel(q_ref, raw_ref, keep_ref, other_ref, gain_ref, gain_far_ref, out_ref):
+def final_kernel(q_ref, raw_ref, keep_ref, other_ref, gain_ref, gain_far_ref, near_ref, far_ref):
     b, c = place()
+    h = ring()
     keep, other = keep_ref[...], other_ref[...]
     m2 = split(
         jnp.concatenate(
-            [jnp.where(c == 0, keep, other), jnp.where(c == 0, other, keep)], axis=1
+            [jnp.where(h == 0, keep, other), jnp.where(h == 0, other, keep)], axis=1
         )
     )
     y = lax.axis_index("y")
@@ -191,8 +203,15 @@
         rows = slice(t * 256, t * 256 + 256)
         raw = raw_ref[rows] + mm2(split(q_ref[rows]), m2, 1, 0)
         mean_sq = jnp.mean(raw * raw, axis=-1, keepdims=True)
-        out = raw * lax.rsqrt(mean_sq + epsilon) * gain
-        out_ref[b if t == 0 else 1 - b] = out.astype(bf16)
+        out = (raw * lax.rsqrt(mean_sq + epsilon) * gain).astype(bf16)
+
+        @pl.when(b == t)
+        def _():
+            near_ref[...] = out
+
+        @pl.when(b != t)
+        def _():
+            far_ref[...] = out
 
 
 def call(kernel, outs, flops, moved, scratch=()):
@@ -205,7 +224,7 @@
     )
 
 
-def swap_perm(flip):
+def pair_swap(flip):
     return [
         ((2 * a + b) * 2 + c, (2 * c + (b ^ flip)) * 2 + a)
         for a in range(2)
@@ -214,52 +233,72 @@
     ]
 
 
+def weight_perm(zs, flip):
+    pairs = []
+    for z in range(zs):
+        zh, z1, z0 = z // 4, z // 2 % 2, z % 2
+        for y in range(4):
+            a, b = y // 2, y % 2
+            for c in range(2):
+                to = (4 * zh + 2 * a + z0) * 8 + (2 * c + (b ^ flip)) * 2 + (z1 ^ z0)
+                pairs.append((z * 8 + y * 2 + c, to))
+    return pairs
+
+
 def body(zs, tokens, weight, gain):
     shape = jax.ShapeDtypeStruct
     b = lax.rem(lax.axis_index("y"), 2)
-    yc = ("y", "core")
+    yc, zyc = ("y", "core"), ("z", "y", "core")
+    core_swap = [(0, 1), (1, 0)]
+    rows, mats = shape((512, HD), f32), lambda n: shape((n, HD, HD), f32)
+    wide = shape((512, 3 * HD), f32)
     first, second = weight[:, :, :HD], weight[:, :, HD:]
     same = jnp.where(b == 0, first, second).transpose(1, 0, 2)
     flip = jnp.where(b == 0, second, first).transpose(1, 0, 2)
-    same = lax.ppermute(same, yc, swap_perm(0))
-    flip = lax.ppermute(flip, yc, swap_perm(1))
-    moved = lax.ppermute(tokens, yc, swap_perm(0))
-    moved, same, flip = lax.optimization_barrier((moved, same, flip))
-    everything = jnp.broadcast_to(moved[None], (16,) + moved.shape)
+    same = lax.ppermute(same, zyc, weight_perm(zs, 0))
+    flip = lax.ppermute(flip, zyc, weight_perm(zs, 1))
+    turn = [(z * 2 + c, z * 2 + (c ^ z % 2)) for z in range(zs) for c in range(2)]
+    tokens = lax.ppermute(tokens, ("z", "core"), turn)
+    everything = jnp.broadcast_to(tokens[None], (16,) + tokens.shape)
+    everything, same, flip = lax.optimization_barrier((everything, same, flip))
     tok = lax.all_to_all(everything, ("y", "x"), 0, 0)
-    own = lax.all_gather(jnp.stack([same, flip]), "z")
-    core_swap = [(0, 1), (1, 0)]
-    other = lax.ppermute(own, "core", core_swap)
-    rows = shape((512, HD), f32)
-    mats = lambda n: shape((n, HD, HD), f32)
-    q, k, v, low, blk, pay = call(
-        project_kernel,
-        (rows, rows, rows, shape((2, 256, 256), f32), mats(3), shape((4, ROWS, HD), f32)),
-        1200 * 10**6,
-        8 * 10**6,
-        [pltpu.VMEM((zs * 128, 3 * HD), bf16)],
-    )(tok, own, other)
+    own = lax.all_gather(
+        jnp.stack([same, flip]), ("z", "core"), axis_index_groups=ring_groups(zs)
+    )
+    scratch = [pltpu.VMEM((zs * 64, 3 * HD), bf16)]
+    send = call(functools.partial(project_kernel, False), wide, 400 * 10**6, 3 * 10**6, scratch)(tok, own)
+    got = lax.ppermute(send, "core", core_swap)
+    keep = call(functools.partial(project_kernel, True), wide, 400 * 10**6, 3 * 10**6, scratch)(tok, own)
+    q, k, v, blk, pay = call(
+        moment_kernel,
+        (rows, rows, rows, mats(3), shape((4, ROWS, HD), f32)),
+        600 * 10**6,
+        3 * 10**6,
+    )(keep, got)
     groups = [[(2 * p + i) * 2 + j for i in range(2) for j in range(2)] for p in range(zs // 2)]
     got = lax.all_to_all(pay, ("z", "core"), 0, 0, axis_index_groups=groups)
     gain, pay = lax.optimization_barrier((gain, pay))
     gain = gain.reshape(2, HD)
     gain_far = lax.ppermute(gain, "core", core_swap)
-    raw = call(local_kernel, rows, 600 * 10**6, 4 * 10**6)(q, v, low, blk)
+    raw = call(local_kernel, rows, 800 * 10**6, 2 * 10**6)(q, k, v, blk)
     total, inner, s_in = call(
-        pair_kernel, (shape((ROWS, HD), f32), mats(2), shape((PACK, HD), f32)), 10**8, 10**6
+        pair_kernel,
+        (shape((ROWS // 2, HD), f32), mats(2), shape((PACK, HD), f32)),
+        10**8,
+        10**6,
+        [pltpu.VMEM((ROWS, HD), f32)],
     )(got)
-    groups = [[2 * p + i for p in range(zs // 2)] for i in range(2)]
-    totals = lax.all_gather(total, "z", axis_index_groups=groups)
+    totals = lax.all_gather(total, ("z", "core"), axis_index_groups=ring_groups(zs))
+    totals = totals.reshape(zs // 2, ROWS, HD)
     s, keep, send = call(
         prior_kernel, (shape((HD, HD), f32), shape((HD, HALF), f32), shape((HD, HALF), f32)), 10**8, 10**6
     )(totals, inner, s_in)
     other_m = lax.ppermute(send, "core", core_swap)
     raw = call(cross_kernel, rows, 500 * 10**6, 2 * 10**6)(q, v, raw, blk, s)
-    out = call(final_kernel, shape((2, 256, HD), bf16), 10**8, 10**6)(
-        q, raw, keep, other_m, gain, gain_far
-    )
-    near = lax.ppermute(out[0], yc, swap_perm(0))
-    far = lax.ppermute(out[1], yc, swap_perm(1))
+    half = shape((256, HD), bf16)
+    near, far = call(final_kernel, (half, half), 10**8, 10**6)(q, raw, keep, other_m, gain, gain_far)
+    near = lax.ppermute(near, yc, pair_swap(0))
+    far = lax.ppermute(far, yc, pair_swap(1))
     left = jnp.where(b == 0, near, far)
     right = jnp.where(b == 0, far, near)
     return jnp.concatenate([left, right], axis=1)

time: 139 us -> 129 us (0.928)
  starting transfers between devices: 50.1 us -> 39.4 us
  local copies, waits for them, and re-layouts: 7.01 us -> 1.55 us
  blocking collectives: 62.8 us -> 66.2 us
    ppermute x6, starting transfers between devices: 33.8 us -> 22.1 us  [the longest x1 5.25 us: body(): same = lax.ppermute(same, zyc, weight_perm(zs, 0))]
    unnamed x16 -> x2, local copies, waits for them, and re-layouts: 5.47 us -> 0.01 us
    all_to_all x1, starting transfers between devices: 4.23 us -> 9.53 us  [body(): tok = lax.all_to_all(everything, ('y', 'x'), 0, 0)]
    ppermute x1, starting transfers between devices: 6.24 us -> 2.02 us  [body(): other_m = lax.ppermute(send, 'core', core_swap)]
    all_gather x2, blocking collectives: 62.8 us -> 66.2 us  [the longest x1 35.4 us: body(): lax.all_gather(jnp.stack([same, flip]), ('z', 'core'), axis_index_groups=...]
    all_to_all x1, waiting for transfers between devices: 1.81 us -> 3.31 us  [body(): got = lax.all_to_all(pay, ('z', 'core'), 0, 0, axis_index_groups=groups)]
    pallas_call x4 -> x6, Pallas kernels: 6.58 us -> 7.34 us  [the longest x1 2.59 us: body(): call(moment_kernel, (rows, rows, rows, mats(3), shape((4, ROWS, HD), f32)...]
  transfers between devices with their start and end apart: 10 -> 10, of which waited for: 4 -> 4; matrix products, arithmetic and copies ran while one was open for 1% -> 1% of each run, Pallas kernels for 3% -> 4%
where the time goes in v2:
time: 129 us; the launch traced here: 128 us
  blocking collectives  66.2 us (51%)
  starting transfers between devices  39.4 us (31%)
  Pallas kernels  9.54 us (7%)
  waiting for transfers between devices  9.45 us (7%)
  local copies, waits for them, and re-layouts  1.55 us (1%)
  other arithmetic  1.45 us (1%)
    all_gather x1, blocking collectives, body(): lax.all_gather(jnp.stack([same, flip]), ('z', 'core'), axis_index_groups=...  35.4 us
    all_gather x1, blocking collectives, body(): lax.all_gather(total, ('z', 'core'), axis_index_groups=ring_groups(zs))  30.8 us
    all_to_all x1, starting transfers between devices, body(): tok = lax.all_to_all(everything, ('y', 'x'), 0, 0)  9.53 us
    ppermute x1, starting transfers between devices, body(): same = lax.ppermute(same, zyc, weight_perm(zs, 0))  5.25 us
    ppermute x1, starting transfers between devices, body(): flip = lax.ppermute(flip, zyc, weight_perm(zs, 1))  5.19 us
    ppermute x1, starting transfers between devices, body(): near = lax.ppermute(near, yc, pair_swap(0))  4.88 us
    ppermute x1, waiting for transfers between devices, body(): far = lax.ppermute(far, yc, pair_swap(1))  4.17 us
    all_to_all x1, starting transfers between devices, body(): got = lax.all_to_all(pay, ('z', 'core'), 0, 0, axis_index_groups=groups)  3.81 us
  transfers between devices with their start and end apart: 10, of which 4 were waited for; matrix products, arithmetic and copies ran while one was open for 1% of the time, Pallas kernels for 4%

profile of v2, /device:TPU:7, one launch (start us, length us, event | category | flops | bytes accessed | tf_op | source)
XLA Modules:
  0.0 127.7 jit_solution(13009517468463495577)
XLA Ops:
  0.0 1.6 %collective-permute-start = (bf16[256,256]{1,0:T(8,128)(2,1)}, bf16[256,256]{1,0:T(8,128)(2,1)S(1)}, u32[]{:S(2)}, u32[]{:S(2)}) collective-permute-start(bf16[256,256]{1,0:T(8,128)(2,1)} %param.3), channel_id=1, source_target_pairs={{0,0},{1,1},{32,33},{33,32},{64,64},{65,65},{96,97},{97,96},{128,1... | collective-permute-start | bytes 393224 | tf_op jit(solution)/shard_map/ppermute | solution.py:261
  1.6 0.8 select_bitcast_fusion
  2.3 5.2 %collective-permute-start.2 = (bf16[3,32,128]{2,1,0:T(8,128)(2,1)S(1)}, bf16[3,32,128]{2,1,0:T(8,128)(2,1)S(1)}, u32[]{:S(2)}, u32[]{:S(2)}) collective-permute-start(bf16[3,32,128]{2,1,0:T(8,128)(2,1)S(1)} %get-tuple-element.41), channel_id=1, source_target_pairs={{0,8},{1,24},{8,0},{9,16},{16,72},{17,88},{24,64},{25,80},{32,41},... | collective-permute-start | bytes 73736 | tf_op jit(solution)/shard_map/ppermute | solution.py:259
  7.5 5.2 %collective-permute-start.1 = (bf16[3,32,128]{2,1,0:T(8,128)(2,1)S(1)}, bf16[3,32,128]{2,1,0:T(8,128)(2,1)S(1)}, u32[]{:S(2)}, u32[]{:S(2)}) collective-permute-start(bf16[3,32,128]{2,1,0:T(8,128)(2,1)S(1)} %get-tuple-element.42), channel_id=1, source_target_pairs={{0,0},{1,16},{8,8},{9,24},{16,64},{17,80},{24,72},{25,88},{32,33},... | collective-permute-start | bytes 73736 | tf_op jit(solution)/shard_map/ppermute | solution.py:258
  12.8 0.0 collective-permute-done.2
  12.8 0.9 collective-permute-done.1
  13.7 0.0 collective-permute-done
  13.7 1.5 %broadcast_in_dim.2 = bf16[16,256,256]{2,1,0:T(8,128)(2,1)} broadcast(bf16[256,256]{1,0:T(8,128)(2,1)S(1)} %collective-permute-done), dimensions={1,2} | broadcast | bytes 2228224 | tf_op jit(solution)/shard_map/broadcast_in_dim | solution.py:262
  15.2 9.5 %all-to-all-start = ((bf16[16,256,256]{2,1,0:T(8,128)(2,1)}), bf16[16,256,256]{2,1,0:T(8,128)(2,1)S(1)}, u32[]{:S(2)}, u32[]{:S(2)}) async-start(bf16[16,256,256]{2,1,0:T(8,128)(2,1)} %broadcast_in_dim.2), calls=%async_computation | async-start | bytes 4194304 | tf_op jit(solution)/shard_map/all_to_all | solution.py:264
  24.8 35.4 %all-gather = bf16[32,3,32,128]{3,2,1,0:T(8,128)(2,1)S(1)} all-gather(bf16[2,3,32,128]{3,2,1,0:T(8,128)(2,1)S(1)} %pad_maximum_fusion.1), channel_id=2, replica_groups={{0,33,64,97,128,161,192,225,256,289,320,353,384,417,448,481},{1,32,65,9..., dimensions={0}, use_global_device_ids=true | all-gather | bytes 835584 | tf_op jit(solution)/shard_map/all_gather | solution.py:265
  60.2 0.0 all-to-all-done.tok
  60.2 0.8 shard_map.38
  61.0 2.6 %collective-permute-start.3 = (f32[512,384]{1,0:T(8,128)S(1)}, f32[512,384]{1,0:T(8,128)S(1)}, u32[]{:S(2)}, u32[]{:S(2)}) collective-permute-start(f32[512,384]{1,0:T(8,128)S(1)} %shard_map.38), channel_id=1, source_target_pairs={{0,1},{1,0},{2,3},{3,2},{4,5},{5,4},{6,7},{7,6},{8,9},{9,8},{10,11... | collective-permute-start | bytes 2359304 | tf_op jit(solution)/shard_map/ppermute | solution.py:270
  63.6 0.8 shard_map.37.keep
  64.4 0.0 copy-start
  64.5 1.0 collective-permute-done.3.got
  65.5 2.6 %shard_map.39 = (f32[512,128]{1,0:T(8,128)S(1)}, f32[512,128]{1,0:T(8,128)S(1)}, f32[512,128]{1,0:T(8,128)S(1)}, f32[3,128,128]{2,1,0:T(8,128)S(1)}, f32[4,224,128]{2,1,0:T(8,128)}) custom-call(f32[512,384]{1,0:T(8,128)S(1)} %shard_map.37.keep, f32[512,384]{1,0:T(8,128)S(1)} %collective-permute-done.3.got), custom_call_target="tpu_custom_call" | custom-call | flops 600000000 | bytes 3000000 | tf_op jit(solution)/shard_map/pallas_call | solution.py:272
  68.1 3.8 %all-to-all-start.1 = ((f32[4,224,128]{2,1,0:T(8,128)}), f32[4,224,128]{2,1,0:T(8,128)S(1)}, u32[]{:S(2)}, u32[]{:S(2)}) async-start(f32[4,224,128]{2,1,0:T(8,128)} %get-tuple-element.29), calls=%async_computation.1 | async-start | bytes 917504 | tf_op jit(solution)/shard_map/all_to_all | solution.py:279
  71.9 0.0 copy-done
  71.9 2.0 %collective-permute-start.5 = (f32[2,128]{1,0:T(2,128)S(1)}, f32[2,128]{1,0:T(2,128)S(1)}, u32[]{:S(2)}, u32[]{:S(2)}) collective-permute-start(f32[2,128]{1,0:T(2,128)S(1)} %bitcast.12), channel_id=1, source_target_pairs={{0,1},{1,0},{2,3},{3,2},{4,5},{5,4},{6,7},{7,6},{8,9},{9,8},{10,11... | collective-permute-start | bytes 3080 | tf_op jit(solution)/shard_map/ppermute | solution.py:282
  73.9 1.9 %shard_map.40.raw_ref = f32[512,128]{1,0:T(8,128)S(1)} custom-call(f32[512,128]{1,0:T(8,128)S(1)} %get-tuple-element.25.q_ref, f32[512,128]{1,0:T(8,128)S(1)} %get-tuple-element.27.k_ref, f32[512,128]{1,0:T(8,128)S(1)} %get-tuple-element.26.v_ref, f32[3,128,128]{2,1,0:T(8,128)S(1)} %get-tuple-element.28.blk_ref), custom_call_target="tpu_custom_call" | custom-call | flops 800000000 | bytes 2000000 | tf_op jit(solution)/shard_map/pallas_call | solution.py:283
  75.7 3.3 %all-to-all-done.1.got = f32[4,224,128]{2,1,0:T(8,128)S(1)} async-done(((f32[4,224,128]{2,1,0:T(8,128)}), f32[4,224,128]{2,1,0:T(8,128)S(1)}, u32[]{:S(2)}, u32[]{:S(2)}) %all-to-all-start.1) | async-done | bytes 458784 | tf_op jit(solution)/shard_map/all_to_all | solution.py:279
  79.0 0.5 shard_map.41
  79.5 30.8 %all-gather.1 = f32[1792,128]{1,0:T(8,128)S(1)} all-gather(f32[112,128]{1,0:T(8,128)S(1)} %get-tuple-element.30), channel_id=3, replica_groups={{0,33,64,97,128,161,192,225,256,289,320,353,384,417,448,481},{1,32,65,9..., dimensions={0}, use_global_device_ids=true | all-gather | bytes 974848 | tf_op jit(solution)/shard_map/all_gather | solution.py:291
  110.3 0.8 shard_map.42
  111.1 2.0 %collective-permute-start.4 = (f32[128,64]{1,0:T(8,128)S(1)}, f32[128,64]{1,0:T(8,128)S(1)}, u32[]{:S(2)}, u32[]{:S(2)}) collective-permute-start(f32[128,64]{1,0:T(8,128)S(1)} %get-tuple-element.35), channel_id=1, source_target_pairs={{0,1},{1,0},{2,3},{3,2},{4,5},{5,4},{6,7},{7,6},{8,9},{9,8},{10,11... | collective-permute-start | bytes 98312 | tf_op jit(solution)/shard_map/ppermute | solution.py:296
  113.2 1.4 %shard_map.43.raw_ref = f32[512,128]{1,0:T(8,128)S(1)} custom-call(f32[512,128]{1,0:T(8,128)S(1)} %get-tuple-element.25.q_ref, f32[512,128]{1,0:T(8,128)S(1)} %get-tuple-element.26.v_ref, f32[512,128]{1,0:T(8,128)S(1)} %shard_map.40.raw_ref, f32[3,128,128]{2,1,0:T(8,128)S(1)} %get-tuple-element.28.blk_ref, f32[128,128]{1,0:T(8,128)S(1)} %get-tuple-element.33.s_ref), custom_call_target="tpu_custom_call" | custom-call | flops 500000000 | bytes 2000000 | tf_op jit(solution)/shard_map/pallas_call | solution.py:297
  114.6 0.0 collective-permute-done.5.gain_far_ref
  114.6 0.0 collective-permute-done.4.other_ref
  114.6 0.7 shard_map.44
  115.3 4.9 %collective-permute-start.6 = (bf16[256,128]{1,0:T(8,128)(2,1)S(1)}, bf16[256,128]{1,0:T(8,128)(2,1)S(1)}, u32[]{:S(2)}, u32[]{:S(2)}) collective-permute-start(bf16[256,128]{1,0:T(8,128)(2,1)S(1)} %get-tuple-element.37), channel_id=1, source_target_pairs={{0,0},{1,16},{8,8},{9,24},{16,1},{17,17},{24,9},{25,25},{2,2},{3,1... | collective-permute-start | bytes 196616 | tf_op jit(solution)/shard_map/ppermute | solution.py:300
  120.2 2.6 %collective-permute-start.7 = (bf16[256,128]{1,0:T(8,128)(2,1)S(1)}, bf16[256,128]{1,0:T(8,128)(2,1)S(1)}, u32[]{:S(2)}, u32[]{:S(2)}) collective-permute-start(bf16[256,128]{1,0:T(8,128)(2,1)S(1)} %get-tuple-element.38), channel_id=1, source_target_pairs={{0,8},{1,24},{8,0},{9,16},{16,9},{17,25},{24,1},{25,17},{2,10},{3,... | collective-permute-start | bytes 196616 | tf_op jit(solution)/shard_map/ppermute | solution.py:301
  122.8 0.0 collective-permute-done.6
  122.8 4.2 %collective-permute-done.7 = bf16[256,128]{1,0:T(8,128)(2,1)S(1)} collective-permute-done((bf16[256,128]{1,0:T(8,128)(2,1)S(1)}, bf16[256,128]{1,0:T(8,128)(2,1)S(1)}, u32[]{:S(2)}, u32[]{:S(2)}) %collective-permute-start.7) | collective-permute-done | bytes 65568 | tf_op jit(solution)/shard_map/ppermute | solution.py:301
  127.0 0.7 pad_maximum_fusion
  (2 shorter events, 0.0 us)
Async XLA Ops:
  0.0 13.7 %collective-permute-start = (bf16[256,256]{1,0:T(8,128)(2,1)}, bf16[256,256]{1,0:T(8,128)(2,1)S(1)}, u32[]{:S(2)}, u32[]{:S(2)}) collective-permute-start(bf16[256,256]{1,0:T(8,128)(2,1)} %param.3), channel_id=1, source_target_pairs={{0,0},{1,1},{32,33},{33,32},{64,64},{65,65},{96,97},{97,96},{128,1... | collective-permute-start | bytes 393224 | tf_op jit(solution)/shard_map/ppermute | solution.py:261
  2.3 10.5 %collective-permute-start.2 = (bf16[3,32,128]{2,1,0:T(8,128)(2,1)S(1)}, bf16[3,32,128]{2,1,0:T(8,128)(2,1)S(1)}, u32[]{:S(2)}, u32[]{:S(2)}) collective-permute-start(bf16[3,32,128]{2,1,0:T(8,128)(2,1)S(1)} %get-tuple-element.41), channel_id=1, source_target_pairs={{0,8},{1,24},{8,0},{9,16},{16,72},{17,88},{24,64},{25,80},{32,41},... | collective-permute-start | bytes 73736 | tf_op jit(solution)/shard_map/ppermute | solution.py:259
  7.5 6.2 %collective-permute-start.1 = (bf16[3,32,128]{2,1,0:T(8,128)(2,1)S(1)}, bf16[3,32,128]{2,1,0:T(8,128)(2,1)S(1)}, u32[]{:S(2)}, u32[]{:S(2)}) collective-permute-start(bf16[3,32,128]{2,1,0:T(8,128)(2,1)S(1)} %get-tuple-element.42), channel_id=1, source_target_pairs={{0,0},{1,16},{8,8},{9,24},{16,64},{17,80},{24,72},{25,88},{32,33},... | collective-permute-start | bytes 73736 | tf_op jit(solution)/shard_map/ppermute | solution.py:258
  15.2 44.9 %all-to-all-start = ((bf16[16,256,256]{2,1,0:T(8,128)(2,1)}), bf16[16,256,256]{2,1,0:T(8,128)(2,1)S(1)}, u32[]{:S(2)}, u32[]{:S(2)}) async-start(bf16[16,256,256]{2,1,0:T(8,128)(2,1)} %broadcast_in_dim.2), calls=%async_computation | async-start | bytes 4194304 | tf_op jit(solution)/shard_map/all_to_all | solution.py:264
  61.0 4.5 %collective-permute-start.3 = (f32[512,384]{1,0:T(8,128)S(1)}, f32[512,384]{1,0:T(8,128)S(1)}, u32[]{:S(2)}, u32[]{:S(2)}) collective-permute-start(f32[512,384]{1,0:T(8,128)S(1)} %shard_map.38), channel_id=1, source_target_pairs={{0,1},{1,0},{2,3},{3,2},{4,5},{5,4},{6,7},{7,6},{8,9},{9,8},{10,11... | collective-permute-start | bytes 2359304 | tf_op jit(solution)/shard_map/ppermute | solution.py:270
  64.4 7.5 %copy-start = (f32[256]{0:T(256)S(1)}, f32[256]{0:T(256)}, u32[]{:S(2)}) copy-start(f32[256]{0:T(256)} %param.5) | copy-start | bytes 3076
  68.1 11.0 %all-to-all-start.1 = ((f32[4,224,128]{2,1,0:T(8,128)}), f32[4,224,128]{2,1,0:T(8,128)S(1)}, u32[]{:S(2)}, u32[]{:S(2)}) async-start(f32[4,224,128]{2,1,0:T(8,128)} %get-tuple-element.29), calls=%async_computation.1 | async-start | bytes 917504 | tf_op jit(solution)/shard_map/all_to_all | solution.py:279
  71.9 42.7 %collective-permute-start.5 = (f32[2,128]{1,0:T(2,128)S(1)}, f32[2,128]{1,0:T(2,128)S(1)}, u32[]{:S(2)}, u32[]{:S(2)}) collective-permute-start(f32[2,128]{1,0:T(2,128)S(1)} %bitcast.12), channel_id=1, source_target_pairs={{0,1},{1,0},{2,3},{3,2},{4,5},{5,4},{6,7},{7,6},{8,9},{9,8},{10,11... | collective-permute-start | bytes 3080 | tf_op jit(solution)/shard_map/ppermute | solution.py:282
  111.1 3.4 %collective-permute-start.4 = (f32[128,64]{1,0:T(8,128)S(1)}, f32[128,64]{1,0:T(8,128)S(1)}, u32[]{:S(2)}, u32[]{:S(2)}) collective-permute-start(f32[128,64]{1,0:T(8,128)S(1)} %get-tuple-element.35), channel_id=1, source_target_pairs={{0,1},{1,0},{2,3},{3,2},{4,5},{5,4},{6,7},{7,6},{8,9},{9,8},{10,11... | collective-permute-start | bytes 98312 | tf_op jit(solution)/shard_map/ppermute | solution.py:296
  115.3 7.5 %collective-permute-start.6 = (bf16[256,128]{1,0:T(8,128)(2,1)S(1)}, bf16[256,128]{1,0:T(8,128)(2,1)S(1)}, u32[]{:S(2)}, u32[]{:S(2)}) collective-permute-start(bf16[256,128]{1,0:T(8,128)(2,1)S(1)} %get-tuple-element.37), channel_id=1, source_target_pairs={{0,0},{1,16},{8,8},{9,24},{16,1},{17,17},{24,9},{25,25},{2,2},{3,1... | collective-permute-start | bytes 196616 | tf_op jit(solution)/shard_map/ppermute | solution.py:300
  120.2 6.8 %collective-permute-start.7 = (bf16[256,128]{1,0:T(8,128)(2,1)S(1)}, bf16[256,128]{1,0:T(8,128)(2,1)S(1)}, u32[]{:S(2)}, u32[]{:S(2)}) collective-permute-start(bf16[256,128]{1,0:T(8,128)(2,1)S(1)} %get-tuple-element.38), channel_id=1, source_target_pairs={{0,8},{1,24},{8,0},{9,16},{16,9},{17,25},{24,1},{25,17},{2,10},{3,... | collective-permute-start | bytes 196616 | tf_op jit(solution)/shard_map/ppermute | solution.py:301
